TPU v7x, 32 devices: a whole 2x2x4 slice. The times are simulated.
32 devices in a mesh: chan: 4 (over x, core), rad: 8 (over z, y).
Axes of the slice: x: 2, y: 2, z: 4, core: 2. Of those that a mesh axis runs over, the one named last changes fastest.
Arguments:
- psi: float32 [2, 768, 128, 128], P(None, 'chan', 'rad'), may hold values from -6 to 6
- k_prev: float32 [2, 768, 128, 128], P(None, 'chan', 'rad'), may hold values from -6 to 6
- gaunt: bfloat16 [4, 768, 768], replicated, may hold values from -0.875 to 0.875
- dipole: bfloat16 [768, 768], replicated, may hold values from -0.875 to 0.875
- kinetic: float32 [128, 128], replicated, as said below
- chan_l: int32 [768, 2], P('chan'), may hold values from 0 to 23
- field_amp: float32 [1], replicated, may hold values from 0.02 to 0.1
Outputs:
- deriv: float32 [2, 768, 128, 128], P(None, 'chan', 'rad')
Inputs may be any that keep to these rules, and one draw needn't show every extreme that they name: `kinetic`: symmetric; zero where the row's and the column's blocks of 16 indices are more than one block apart.
All inputs are finite; a program needn't handle non-finite values.
Results may differ from a plain program's by a relative error of at most 0.00037.
Values may be sent and summed in bfloat16 or wider, within the bound.
A program may use at most 64 MiB of HBM per device.

v0:
```python
import jax
import jax.numpy as jnp
from jax import lax
from jax.sharding import PartitionSpec as P


def extended(array, sides, width):
    for axis, dim in sides:
        peers, length = (lax.axis_size(axis), array.shape[dim])
        up = [(i, (i + 1) % peers) for i in range(peers - 1)]
        down = [(j, i) for i, j in up]
        last = lax.slice_in_dim(array, length - width, length, axis=dim)
        initial = lax.slice_in_dim(array, 0, width, axis=dim)
        before = lax.ppermute(last, axis, up)
        after = lax.ppermute(initial, axis, down)
        array = jnp.concatenate([before, array, after], axis=dim)
    return array


def on_device(psi, k_prev, gaunt, dipole, kinetic, chan_l, field_amp):
    highest = lax.Precision.HIGHEST
    section = psi + 0.5 * k_prev
    local_chan = section.shape[1]
    rows = section.shape[2]
    width = section.shape[3]
    rad_at = lax.axis_index("rad")
    first_r = (
        1.0 + 8.0 * (rad_at * rows + jnp.arange(rows, dtype=jnp.int32)).astype(jnp.float32) / width
    )
    second_r = 1.0 + 8.0 * jnp.arange(width, dtype=jnp.float32) / width
    along_r2 = jnp.einsum("acij,kj->acik", section, kinetic, precision=highest)
    padded = extended(section.astype(jnp.bfloat16), (("rad", 2),), rows).astype(section.dtype)
    band = lax.dynamic_slice_in_dim(kinetic, rad_at * rows, rows, 0)
    widened = jnp.pad(band, ((0, 0), (rows, rows)))
    local_band = lax.dynamic_slice_in_dim(widened, rad_at * rows, 3 * rows, 1)
    along_r1 = jnp.einsum("ij,acjk->acik", local_band, padded, precision=highest)
    lvals = chan_l.astype(jnp.float32)
    first_l = lvals[:, 0] * (lvals[:, 0] + 1.0)
    second_l = lvals[:, 1] * (lvals[:, 1] + 1.0)
    potential = (
        first_l[:, None, None] / (2.0 * first_r * first_r)[None, :, None]
        + second_l[:, None, None] / (2.0 * second_r * second_r)[None, None, :]
        - 2.0 / first_r[None, :, None]
        - 2.0 / second_r[None, None, :]
    )
    sent = section.astype(jnp.bfloat16).reshape(2, local_chan, rows * width)
    chan_at = lax.axis_index("chan")
    block = lax.all_to_all(sent, "chan", split_axis=2, concat_axis=1, tiled=True)
    count = block.shape[2]
    place = chan_at * count + jnp.arange(count, dtype=jnp.int32)
    row_r = 1.0 + 8.0 * (rad_at * rows + place // width).astype(jnp.float32) / width
    col_r = 1.0 + 8.0 * (place % width).astype(jnp.float32) / width
    far = jnp.maximum(row_r, col_r)
    near = jnp.minimum(row_r, col_r)
    inverse = 1.0 / far
    ratio = near * inverse
    power = inverse
    total = jnp.zeros(block.shape, jnp.float32)
    for order in range(gaunt.shape[0]):
        mixed = jnp.einsum("cd,adq->acq", gaunt[order], block, preferred_element_type=jnp.float32)
        total = total + power[None, None, :] * mixed
        power = power * ratio
    mixed = jnp.einsum("cd,adq->acq", dipole, block, preferred_element_type=jnp.float32)
    total = total + (field_amp[0] * (row_r + col_r))[None, None, :] * mixed
    coupled = lax.all_to_all(
        total.astype(jnp.bfloat16), "chan", split_axis=1, concat_axis=2, tiled=True
    )
    coupled = coupled.reshape(coupled.shape[0], local_chan, rows, width)
    ham = along_r1 + along_r2 + potential[None] * section + coupled.astype(jnp.float32)
    return jnp.stack([ham[1], -ham[0]])


def solution(mesh):
    placed = (
        P(None, "chan", "rad", None),
        P(None, "chan", "rad", None),
        P(),
        P(),
        P(),
        P("chan", None),
        P(),
    )
    return jax.shard_map(
        on_device,
        mesh=mesh,
        in_specs=placed,
        out_specs=P(None, "chan", "rad", None),
        check_vma=False,
    )
```

profile of v0, /device:TPU:20, one launch (start us, length us, event | category | flops | bytes accessed | tf_op | source)
XLA Modules:
  0.0 109.9 jit_solution(6782526796202875997)
XLA Ops:
  0.0 0.0 copy-start
  0.0 4.5 %fusion.45 = bf16[2,192,16,128]{3,2,1,0:T(8,128)(2,1)} fusion(f32[2,192,16,128]{3,2,1,0:T(8,128)} %param.7, f32[2,192,16,128]{3,2,1,0:T(8,128)} %param.8), kind=kLoop, calls=%fused_computation.70 | loop fusion | flops 2359296 | bytes 7864320 | tf_op jit(solution)/shard_map/convert_element_type | solution.py:32
  4.5 0.0 copy-start.2
  4.5 0.0 copy-start.1
  4.5 3.5 %collective-permute-start = (bf16[2,192,16,128]{3,2,1,0:T(8,128)(2,1)}, bf16[2,192,16,128]{3,2,1,0:T(8,128)(2,1)}, u32[]{:S(2)}, u32[]{:S(2)}) collective-permute-start(bf16[2,192,16,128]{3,2,1,0:T(8,128)(2,1)} %fusion.45), channel_id=1, source_target_pairs={{0,1},{1,2},{2,3},{3,4},{4,5},{5,6},{6,7},{8,9},{9,10},{10,11},{11... | collective-permute-start | bytes 4718600 | tf_op jit(solution)/shard_map/ppermute | solution.py:14
  8.0 2.4 %collective-permute-start.1 = (bf16[2,192,16,128]{3,2,1,0:T(8,128)(2,1)}, bf16[2,192,16,128]{3,2,1,0:T(8,128)(2,1)}, u32[]{:S(2)}, u32[]{:S(2)}) collective-permute-start(bf16[2,192,16,128]{3,2,1,0:T(8,128)(2,1)} %fusion.45), channel_id=1, source_target_pairs={{1,0},{2,1},{3,2},{4,3},{5,4},{6,5},{7,6},{9,8},{10,9},{11,10},{12... | collective-permute-start | bytes 4718600 | tf_op jit(solution)/shard_map/ppermute | solution.py:15
  10.5 4.6 %copy.43 = bf16[2,192,16,128]{1,0,3,2:T(2,128)(2,1)} copy(bf16[2,192,16,128]{3,2,1,0:T(8,128)(2,1)} %fusion.45) | data formatting | bytes 3145728 | tf_op jit(solution)/shard_map/reshape | solution.py:46
  15.1 3.6 %all-to-all-start = ((bf16[2,192,2048]{1,0,2:T(2,128)(2,1)}), bf16[2,192,2048]{1,0,2:T(2,128)(2,1)S(1)}, u32[]{:S(2)}, u32[]{:S(2)}) async-start(bf16[2,192,2048]{1,0,2:T(2,128)(2,1)} %bitcast.55), calls=%async_computation | async-start | bytes 4194304 | tf_op jit(solution)/shard_map/all_to_all | solution.py:48
  19.4 0.0 copy-done.2
  19.5 0.0 copy-done.1
  19.6 0.1 broadcast_divide_fusion.1
  19.7 24.7 %all-to-all-done = bf16[2,192,2048]{1,0,2:T(2,128)(2,1)S(1)} async-done(((bf16[2,192,2048]{1,0,2:T(2,128)(2,1)}), bf16[2,192,2048]{1,0,2:T(2,128)(2,1)S(1)}, u32[]{:S(2)}, u32[]{:S(2)}) %all-to-all-start) | async-done | bytes 1572896 | tf_op jit(solution)/shard_map/all_to_all | solution.py:48
  44.4 4.6 %copy.44 = bf16[2,192,4,512]{3,2,1,0:T(4,128)(2,1)} copy(bf16[2,192,4,512]{1,0,3,2:T(2,128)(2,1)S(1)} %bitcast.54) | data formatting | bytes 3145728 | tf_op jit(solution)/shard_map/all_to_all | solution.py:48
  49.0 0.0 slice-start
  49.0 1.9 %copy.27 = bf16[2,4,192,512]{3,2,1,0:T(8,128)(2,1)S(1)} copy(bf16[2,4,192,512]{3,1,2,0:T(4,128)(2,1)} %bitcast.56) | data formatting | bytes 3145728 | tf_op jit(solution)/shard_map/all_to_all | solution.py:48
  50.9 0.0 slice-start.1
  50.9 2.8 %fusion.12 = f32[2,512,768]{2,1,0:T(8,128)S(1)} fusion(bf16[2,768,512]{2,1,0:T(8,128)(2,1)S(1)} %bitcast.58, bf16[4,768,768]{2,1,0:T(8,128)(2,1)} %param.9), kind=kOutput, calls=%fused_computation.17 | convolution fusion | flops 1207959552 | bytes 5898240 | tf_op jit(solution)/shard_map/cd,adq->acq/dot_general | solution.py:60
  53.7 2.7 %fusion.14 = f32[2,512,768]{2,1,0:T(8,128)S(1)} fusion(bf16[2,768,512]{2,1,0:T(8,128)(2,1)S(1)} %bitcast.59, bf16[4,768,768]{2,1,0:T(8,128)(2,1)} %param.9), kind=kOutput, calls=%fused_computation.19 | convolution fusion | flops 1207959552 | bytes 5898240 | tf_op jit(solution)/shard_map/cd,adq->acq/dot_general | solution.py:60
  56.4 0.0 slice-done
  56.4 0.0 slice-done.1
  56.4 1.4 %fusion.16 = f32[2,512,768]{2,1,0:T(8,128)S(1)} fusion(bf16[2,768,512]{2,1,0:T(8,128)(2,1)S(1)} %bitcast.60, bf16[4,768,768]{2,1,0:T(8,128)(2,1)S(1)} %bitcast.66), kind=kOutput, calls=%fused_computation.21 | convolution fusion | flops 1207959552 | bytes 5898240 | tf_op jit(solution)/shard_map/cd,adq->acq/dot_general | solution.py:60
  57.8 1.4 %fusion.18 = f32[2,512,768]{2,1,0:T(8,128)S(1)} fusion(bf16[2,768,512]{2,1,0:T(8,128)(2,1)S(1)} %bitcast.61, bf16[4,768,768]{2,1,0:T(8,128)(2,1)S(1)} %bitcast.66), kind=kOutput, calls=%fused_computation.23 | convolution fusion | flops 1207959552 | bytes 5898240 | tf_op jit(solution)/shard_map/cd,adq->acq/dot_general | solution.py:60
  59.3 0.0 copy-done
  59.3 2.7 %fusion.10 = bf16[2,768,512]{1,2,0:T(8,128)(2,1)S(1)} fusion(bf16[2,768,512]{2,1,0:T(8,128)(2,1)S(1)} %bitcast.62, f32[512]{0:T(512)S(1)} %get-tuple-element.9, f32[2,512,768]{2,1,0:T(8,128)S(1)} %fusion.12, f32[512]{0:T(512)S(1)} %get-tuple-element.12, f32[2,512,768]{2,1,0:T(8,128)S(1)} %fusion.14, f32[512]{0:T(512)S(1)} %fusion.40, ...), kind=kOutput, calls=%fused_computation.15 | convolution fusion | flops 1215823872 | bytes 16918528 | tf_op jit(solution)/shard_map/cd,adq->acq/dot_general | solution.py:63
  62.0 3.0 %copy.33 = bf16[2,768,512]{2,0,1:T(2,128)(2,1)} copy(bf16[2,768,512]{1,2,0:T(8,128)(2,1)S(1)} %fusion.10) | data formatting | bytes 3145728 | tf_op jit(solution)/shard_map/convert_element_type | solution.py:66
  65.0 4.5 %all-to-all-start.1 = ((bf16[2,768,512]{2,0,1:T(2,128)(2,1)}), bf16[2,768,512]{2,0,1:T(2,128)(2,1)}, u32[]{:S(2)}, u32[]{:S(2)}) async-start(bf16[2,768,512]{2,0,1:T(2,128)(2,1)} %copy.33), calls=%async_computation.1 | async-start | bytes 3145728 | tf_op jit(solution)/shard_map/all_to_all | solution.py:65
  69.5 0.1 broadcast_divide_fusion
  69.6 0.5 subtract_subtract_fusion
  70.1 5.9 %fusion.24 = f32[2,192,16,128]{3,2,1,0:T(8,128)} fusion(f32[128,128]{1,0:T(8,128)S(1)} %copy-done.1, f32[2,192,16,128]{3,2,1,0:T(8,128)} %param.7, f32[2,192,16,128]{3,2,1,0:T(8,128)} %param.8), kind=kOutput, calls=%fused_computation.29 | convolution fusion | flops 1209532416 | bytes 9502720 | tf_op jit(solution)/shard_map/acij,kj->acik/dot_general | solution.py:31
  76.0 13.5 %all-to-all-done.1 = bf16[2,768,512]{2,0,1:T(2,128)(2,1)} async-done(((bf16[2,768,512]{2,0,1:T(2,128)(2,1)}), bf16[2,768,512]{2,0,1:T(2,128)(2,1)}, u32[]{:S(2)}, u32[]{:S(2)}) %all-to-all-start.1) | async-done | bytes 1572896 | tf_op jit(solution)/shard_map/all_to_all | solution.py:65
  89.5 1.7 %copy.34 = bf16[2,768,512]{2,1,0:T(8,128)(2,1)S(1)} copy(bf16[2,768,512]{2,0,1:T(2,128)(2,1)} %all-to-all-done.1) | data formatting | bytes 3145728 | tf_op jit(solution)/shard_map/all_to_all | solution.py:65
  91.1 0.4 convert_bitcast_fusion
  91.6 3.7 %copy.35 = f32[2,192,4,512]{3,2,1,0:T(4,128)} copy(f32[2,192,4,512]{3,1,2,0:T(8,128)S(1)} %convert_bitcast_fusion) | data formatting | bytes 6291456 | tf_op jit(solution)/shard_map/convert_element_type | solution.py:69
  95.3 5.1 %reshape.171 = f32[2,192,16,128]{3,2,1,0:T(8,128)} reshape(f32[2,192,4,512]{3,2,1,0:T(4,128)} %copy.35) | data formatting | bytes 6291456 | tf_op jit(solution)/shard_map/convert_element_type | solution.py:69
  100.3 0.0 copy-start.3
  100.4 0.0 collective-permute-done
  100.4 0.0 collective-permute-done.1
  100.4 7.6 %fusion.7 = f32[2,192,16,128]{3,2,1,0:T(8,128)S(1)} fusion(f32[2,192,16,128]{3,2,1,0:T(8,128)} %reshape.171, f32[2,192,16,128]{3,2,1,0:T(8,128)} %fusion.24, bf16[2,192,16,128]{3,2,1,0:T(8,128)(2,1)} %collective-permute-done.1, bf16[2,192,16,128]{3,2,1,0:T(8,128)(2,1)} %fusion.45, bf16[2,192,16,128]{3,2,1,0:T(8,128)(2,1)} %collective-permute-done, ...), kind=kOutput, calls=%fused_computation.10 | convolution fusion | flops 471859200 | bytes 22028292 | tf_op jit(solution)/shard_map/ij,acjk->acik/dot_general | solution.py:36
  107.9 0.0 copy-done.3
  107.9 0.3 fusion.46
  108.2 0.0 copy-start.4
  108.2 1.7 %copy-done.4 = f32[2,192,16,128]{3,2,1,0:T(8,128)} copy-done((f32[2,192,16,128]{3,2,1,0:T(8,128)}, f32[2,192,16,128]{3,2,1,0:T(8,128)S(1)}, u32[]{:S(2)}) %copy-start.4) | copy-done | bytes 3145752
  (14 shorter events, 0.1 us)
Async XLA Ops:
  0.0 59.3 %copy-start = (bf16[768,768]{1,0:T(8,128)(2,1)S(1)}, bf16[768,768]{1,0:T(8,128)(2,1)}, u32[]{:S(2)}) copy-start(bf16[768,768]{1,0:T(8,128)(2,1)} %param.10) | copy-start | bytes 3538948
  4.5 15.0 %copy-start.2 = (s32[192,2]{0,1:T(2,128)S(1)}, s32[192,2]{0,1:T(2,128)}, u32[]{:S(2)}) copy-start(s32[192,2]{0,1:T(2,128)} %param.12) | copy-start | bytes 4612
  4.5 15.1 %copy-start.1 = (f32[128,128]{1,0:T(8,128)S(1)}, f32[128,128]{1,0:T(8,128)}, u32[]{:S(2)}) copy-start(f32[128,128]{1,0:T(8,128)} %param.11) | copy-start | bytes 196612
  4.5 95.9 %collective-permute-start = (bf16[2,192,16,128]{3,2,1,0:T(8,128)(2,1)}, bf16[2,192,16,128]{3,2,1,0:T(8,128)(2,1)}, u32[]{:S(2)}, u32[]{:S(2)}) collective-permute-start(bf16[2,192,16,128]{3,2,1,0:T(8,128)(2,1)} %fusion.45), channel_id=1, source_target_pairs={{0,1},{1,2},{2,3},{3,4},{4,5},{5,6},{6,7},{8,9},{9,10},{10,11},{11... | collective-permute-start | bytes 4718600 | tf_op jit(solution)/shard_map/ppermute | solution.py:14
  8.0 92.3 %collective-permute-start.1 = (bf16[2,192,16,128]{3,2,1,0:T(8,128)(2,1)}, bf16[2,192,16,128]{3,2,1,0:T(8,128)(2,1)}, u32[]{:S(2)}, u32[]{:S(2)}) collective-permute-start(bf16[2,192,16,128]{3,2,1,0:T(8,128)(2,1)} %fusion.45), channel_id=1, source_target_pairs={{1,0},{2,1},{3,2},{4,3},{5,4},{6,5},{7,6},{9,8},{10,9},{11,10},{12... | collective-permute-start | bytes 4718600 | tf_op jit(solution)/shard_map/ppermute | solution.py:15
  15.1 29.2 %all-to-all-start = ((bf16[2,192,2048]{1,0,2:T(2,128)(2,1)}), bf16[2,192,2048]{1,0,2:T(2,128)(2,1)S(1)}, u32[]{:S(2)}, u32[]{:S(2)}) async-start(bf16[2,192,2048]{1,0,2:T(2,128)(2,1)} %bitcast.55), calls=%async_computation | async-start | bytes 4194304 | tf_op jit(solution)/shard_map/all_to_all | solution.py:48
  49.0 7.4 %slice-start = ((s8[4718592]{0:T(1024)(128)(4,1)}), s8[4194304]{0:T(1024)(128)(4,1)S(1)}, s32[]{:S(2)}) async-start(s8[4718592]{0:T(1024)(128)(4,1)} %bitcast.65), calls=%async_computation.2 | async-start | bytes 8388608
  50.9 5.5 %slice-start.1 = ((s8[4718592]{0:T(1024)(128)(4,1)}), s8[524288]{0:T(1024)(128)(4,1)S(1)}, s32[]{:S(2)}) async-start(s8[4718592]{0:T(1024)(128)(4,1)} %bitcast.65), calls=%async_computation.3 | async-start | bytes 1048576
  65.0 24.5 %all-to-all-start.1 = ((bf16[2,768,512]{2,0,1:T(2,128)(2,1)}), bf16[2,768,512]{2,0,1:T(2,128)(2,1)}, u32[]{:S(2)}, u32[]{:S(2)}) async-start(bf16[2,768,512]{2,0,1:T(2,128)(2,1)} %copy.33), calls=%async_computation.1 | async-start | bytes 3145728 | tf_op jit(solution)/shard_map/all_to_all | solution.py:65
  100.3 7.6 %copy-start.3 = (f32[2,192,16,128]{3,2,1,0:T(8,128)S(1)}, f32[2,192,16,128]{3,2,1,0:T(8,128)}, u32[]{:S(2)}) copy-start(f32[2,192,16,128]{3,2,1,0:T(8,128)} %custom-call) | copy-start | bytes 9437188
  108.2 1.7 %copy-start.4 = (f32[2,192,16,128]{3,2,1,0:T(8,128)}, f32[2,192,16,128]{3,2,1,0:T(8,128)S(1)}, u32[]{:S(2)}) copy-start(f32[2,192,16,128]{3,2,1,0:T(8,128)S(1)} %get-tuple-element.17) | copy-start | bytes 9437188
where the time goes:
time: 112 us; the launch traced here: 110 us
  waiting for transfers between devices  38.1 us (34%)
  local copies, waits for them, and re-layouts  26.3 us (23%)
  matrix products  24.4 us (22%)
  starting transfers between devices  14.1 us (13%)
  other arithmetic  5.95 us (5%)
    all_to_all x1, waiting for transfers between devices, on_device(): lax.all_to_all(sent, 'chan', split_axis=2, concat_axis=1, tiled=True)  24.7 us
    all_to_all x1, waiting for transfers between devices, on_device(): lax.all_to_all(total.astype(jnp.bfloat16), 'chan', split_axis=1, concat_a...  13.5 us
    convert_element_type x2, local copies, waits for them, and re-layouts, on_device(): coupled.astype(jnp.float32)  8.79 us
    dot_general x4, matrix products, on_device(): jnp.einsum('cd,adq->acq', gaunt[order], block, preferred_element_type=jnp...  8.34 us
    dot_general x1, matrix products, on_device(): jnp.einsum('ij,acjk->acik', local_band, padded, precision=highest)  7.55 us
    all_to_all x2, local copies, waits for them, and re-layouts, on_device(): lax.all_to_all(sent, 'chan', split_axis=2, concat_axis=1, tiled=True)  6.5 us
    dot_general x1, matrix products, on_device(): along_r2 = jnp.einsum('acij,kj->acik', section, kinetic, precision=highest)  5.87 us
    reshape x1, local copies, waits for them, and re-layouts, on_device(): sent = section.astype(jnp.bfloat16).reshape(2, local_chan, rows * width)  4.64 us
  transfers between devices with their start and end apart: 4, of which 2 were waited for; matrix products, arithmetic and copies ran while one was open for 39% of the time, Pallas kernels for 0%

commit v1 on v0

--- a/solution.py
+++ b/solution.py
@@ -1,6 +1,10 @@
+import functools
+
 import jax
 import jax.numpy as jnp
 from jax import lax
+from jax.experimental import pallas as pl
+from jax.experimental.pallas import tpu as pltpu
 from jax.sharding import PartitionSpec as P
 
 
@@ -70,6 +74,439 @@
     return jnp.stack([ham[1], -ham[0]])
 
 
+MESH = pl.DeviceIdType.MESH
+GROUP = 16
+
+
+def split_bf16(value):
+    high = value.astype(jnp.bfloat16)
+    return high, (value - high.astype(jnp.float32)).astype(jnp.bfloat16)
+
+
+def fused_kernel(
+    peers,
+    rads,
+    psi,
+    k_prev,
+    gaunt,
+    dipole,
+    kin,
+    chan_l,
+    field,
+    out,
+    pbuf,
+    kbuf,
+    sec,
+    xg,
+    halo,
+    acc,
+    acc1,
+    weights,
+    wr1,
+    kk,
+    lmul,
+    langle,
+    load_sem,
+    weight_sem,
+    xs,
+    xr,
+    cs,
+    cr,
+    fs,
+    fr,
+    ys,
+    yr,
+    zs,
+    zr,
+    store_sem,
+):
+    rows, chans, lanes = sec.shape
+    width = lanes // 2
+    orders = weights.shape[0]
+    chips = peers // 2
+    halves = rows // 8
+    quarter = rows // 4
+    span = chans // 4
+    chan_at = lax.axis_index("chan")
+    rad_at = lax.axis_index("rad")
+    core = chan_at % 2
+    chip = chan_at // 2
+    partner = chan_at + 1 - 2 * core
+    minor = rad_at % 2
+    other = rad_at + 1 - 2 * minor
+    ahead = rad_at + 2 - 4 * minor
+    behind = rad_at - 2 + 4 * minor
+    has_ahead = jnp.logical_and(ahead >= 0, ahead < rads)
+    has_behind = jnp.logical_and(behind >= 0, behind < rads)
+    near_slot = 1 - minor
+    far_slot = minor
+
+    def block(owner):
+        return pl.ds(pl.multiple_of(owner * chans, GROUP), chans)
+
+    def chip_peer(step):
+        return lax.rem(chip + step, chips) * 2 + core
+
+    def chip_source(step):
+        return lax.rem(chip - step + chips, chips) * 2 + core
+
+    def load(which, half, part):
+        source, target = ((psi, pbuf), (k_prev, kbuf))[which]
+        return pltpu.make_async_copy(
+            source.at[part, :, pl.ds(half * 8, 8), :],
+            target.at[half, part],
+            load_sem.at[which, half, part],
+        )
+
+    def load_weight(order):
+        source = gaunt.at[order] if order < orders - 1 else dipole
+        return pltpu.make_async_copy(
+            source.at[block(chan_at), :], weights.at[order], weight_sem.at[order]
+        )
+
+    def store(half, part):
+        return pltpu.make_async_copy(
+            pbuf.at[half, part],
+            out.at[part, :, pl.ds(half * 8, 8), :],
+            store_sem.at[half, part],
+        )
+
+    def remote(ref, send, recv, target):
+        return pltpu.make_async_remote_copy(
+            src_ref=ref[0],
+            dst_ref=ref[1],
+            send_sem=send,
+            recv_sem=recv,
+            device_id=target,
+            device_id_type=MESH,
+        )
+
+    def chip_copy(step, row, owner):
+        view = xg.at[row, block(owner), :]
+        return remote(
+            (view, view), xs.at[step - 1, row], xr.at[step - 1, row], {"chan": chip_peer(step)}
+        )
+
+    def core_copy(row, owner):
+        view = xg.at[row, block(owner), :]
+        return remote((view, view), cs.at[row], cr.at[row], {"chan": partner})
+
+    def relay_copy(step, row, owner):
+        view = xg.at[row, block(owner), :]
+        return remote((view, view), fs.at[step - 1, row], fr.at[step - 1, row], {"chan": partner})
+
+    def piece(index):
+        row = pl.ds(pl.multiple_of((index // 4) * quarter, quarter), quarter)
+        first = pl.multiple_of((index % 4) * span, GROUP)
+        return row, first
+
+    def own_piece(index):
+        row, first = piece(index)
+        start = pl.multiple_of(chan_at * chans + first, GROUP)
+        return xg.at[row, pl.ds(start, span), :]
+
+    def halo_piece(slot, index):
+        row, first = piece(index)
+        return halo.at[slot, row, pl.ds(first, span), :]
+
+    def side_copy(index):
+        return remote(
+            (own_piece(index), halo_piece(minor, index)), ys.at[index], yr.at[index], {"rad": other}
+        )
+
+    def far_copy(index):
+        return remote(
+            (halo_piece(near_slot, index), halo_piece(minor, index)),
+            zs.at[index],
+            zr.at[index],
+            {"rad": ahead},
+        )
+
+    for half in range(halves):
+        for part in range(2):
+            for which in range(2):
+                load(which, half, part).start()
+    for order in range(orders):
+        load_weight(order).start()
+
+    barrier = pltpu.get_barrier_semaphore()
+    for step in range(1, chips):
+        pl.semaphore_signal(
+            barrier, inc=1, device_id={"chan": chip_peer(step)}, device_id_type=MESH
+        )
+    pl.semaphore_signal(barrier, inc=1, device_id={"chan": partner}, device_id_type=MESH)
+    pl.semaphore_signal(barrier, inc=1, device_id={"rad": other}, device_id_type=MESH)
+
+    @pl.when(has_ahead)
+    def _():
+        pl.semaphore_signal(barrier, inc=1, device_id={"rad": ahead}, device_id_type=MESH)
+
+    @pl.when(has_behind)
+    def _():
+        pl.semaphore_signal(barrier, inc=1, device_id={"rad": behind}, device_id_type=MESH)
+
+    pl.semaphore_wait(
+        barrier, chips + 1 + has_ahead.astype(jnp.int32) + has_behind.astype(jnp.int32)
+    )
+
+    def send_row(row):
+        for step in range(1, chips):
+            chip_copy(step, row, chan_at).start()
+        core_copy(row, chan_at).start()
+
+    def send_side(first):
+        for index in range(4):
+            side_copy(first * 4 + index).start()
+
+    for half in range(halves):
+        for part in range(2):
+            for which in range(2):
+                load(which, half, part).wait()
+        for row in range(half * 8, half * 8 + 8):
+            for part in range(2):
+                place = (pl.ds(row % 8, chans, stride=8), slice(None))
+                value = (
+                    pbuf.at[half, part].reshape(chans * 8, width)[place]
+                    + 0.5 * kbuf.at[half, part].reshape(chans * 8, width)[place]
+                )
+                cut = slice(part * width, (part + 1) * width)
+                sec[row, :, cut] = value
+                xg[row, block(chan_at), cut] = value.astype(jnp.bfloat16)
+            if row >= 1:
+                send_row(row - 1)
+                if row % quarter == 0:
+                    send_side(row // quarter - 1)
+
+    kin_high, kin_low = split_bf16(kin[...])
+    both = jnp.concatenate([kin_high, kin_low], axis=1)
+    kk[0:width, :] = both
+    kk[width : 2 * width, :] = both
+    send_row(rows - 1)
+    send_side(3)
+
+    band = kin[pl.ds(pl.multiple_of(rad_at * rows, rows), rows), :]
+    size = rows * GROUP
+    tall = jnp.broadcast_to(band[:, None, :], (rows, GROUP, width)).reshape(size, width)
+    tall_high, tall_low = split_bf16(tall)
+    at_row = lax.broadcasted_iota(jnp.int32, (size, size), 0)
+    at_col = lax.broadcasted_iota(jnp.int32, (size, size), 1)
+    same = (at_row % GROUP) == (at_col % GROUP)
+    from_j = lax.broadcasted_iota(jnp.int32, (width, size), 0)
+    to_col = lax.broadcasted_iota(jnp.int32, (width, size), 1)
+    for side in range(3):
+        pick = from_j == (rad_at + side - 1) * rows + to_col // GROUP
+        pick = jnp.where(pick, 1.0, 0.0).astype(jnp.bfloat16)
+        for level, source in enumerate((tall_high, tall_low)):
+            wide = jnp.dot(source, pick, preferred_element_type=jnp.float32)
+            wr1[side, level * size : (level + 1) * size, :] = jnp.where(same, wide, 0.0).astype(
+                jnp.bfloat16
+            )
+
+    @pl.when(jnp.logical_not(has_behind))
+    def _():
+        halo[far_slot] = jnp.zeros(halo.shape[1:], halo.dtype)
+
+    second_r = 1.0 + 8.0 * (
+        lax.broadcasted_iota(jnp.int32, (1, lanes), 1) % width
+    ).astype(jnp.float32) / width
+    inner_r = second_r[:, :width]
+    lvals = chan_l[...].astype(jnp.float32)
+    lvals = lvals * (lvals + 1.0)
+    lmul[...] = jnp.broadcast_to(lvals[:, 0:1], (chans, width))
+    langle[...] = lvals[:, 1:2] / (2.0 * inner_r * inner_r) - 2.0 / inner_r
+
+    def radius(row):
+        place = jnp.full((1, lanes), rad_at * rows + row, jnp.int32)
+        return 1.0 + 8.0 * place.astype(jnp.float32) / width
+
+    for order in range(orders):
+        load_weight(order).wait()
+
+    def local_row(row):
+        first_r = radius(row)[:, :width]
+        scale = 1.0 / (2.0 * first_r * first_r)
+        shift = 2.0 / first_r
+        potential = lmul[...] * scale + langle[...] - shift
+        for part in range(2):
+            cut = slice(part * width, (part + 1) * width)
+            value = sec[row, :, cut]
+            high = xg[row, block(chan_at), cut]
+            low = (value - high.astype(jnp.float32)).astype(jnp.bfloat16)
+            both = jnp.dot(
+                jnp.concatenate([high, low], axis=1), kk[...], preferred_element_type=jnp.float32
+            )
+            acc[row, :, cut] = both[:, :width] + both[:, width:] + potential * value
+
+    def mix(side, value):
+        both = jnp.dot(wr1[side], value, preferred_element_type=jnp.float32)
+        return both[:size] + both[size:]
+
+    def own_group(index):
+        first = pl.multiple_of(index * GROUP, GROUP)
+        start = pl.multiple_of(chan_at * chans + first, GROUP)
+        high = xg[:, pl.ds(start, GROUP), :].reshape(size, lanes)
+        value = sec[:, pl.ds(first, GROUP), :].reshape(size, lanes)
+        low = (value - high.astype(jnp.float32)).astype(jnp.bfloat16)
+        total = mix(1, high) + jnp.dot(
+            wr1[1, 0:size, :], low, preferred_element_type=jnp.float32
+        )
+        acc1[:, pl.ds(first, GROUP), :] = total.reshape(rows, GROUP, lanes)
+
+    def side_group(index):
+        first = pl.multiple_of(index * GROUP, GROUP)
+        cut = pl.ds(first, GROUP)
+        total = mix(0, halo[0, :, cut, :].reshape(size, lanes)) + mix(
+            2, halo[1, :, cut, :].reshape(size, lanes)
+        )
+        acc1[:, cut, :] = acc1[:, cut, :] + total.reshape(rows, GROUP, lanes)
+
+    def couple(row):
+        first_r = radius(row)
+        inverse = 1.0 / jnp.maximum(first_r, second_r)
+        ratio = jnp.minimum(first_r, second_r) * inverse
+        factors = [inverse]
+        for _ in range(orders - 2):
+            factors.append(factors[-1] * ratio)
+        factors.append(field[0] * (first_r + second_r))
+        step = chans // 2
+        for first in range(0, chans, step):
+            total = jnp.zeros((step, lanes), jnp.float32)
+            for order in range(orders):
+                total = total + factors[order] * jnp.dot(
+                    weights[order, first : first + step, :],
+                    xg[row],
+                    preferred_element_type=jnp.float32,
+                )
+            acc[row, first : first + step, :] = acc[row, first : first + step, :] + total.astype(
+                jnp.bfloat16
+            ).astype(jnp.float32)
+
+    def take_row(row):
+        core_copy(row, partner).wait_recv()
+        for step in range(1, chips):
+            relay_copy(step, row, chip_source(step) + 1 - 2 * core).wait_recv()
+        couple(row)
+
+    def main(row, carry):
+        @pl.when(row < chans // GROUP)
+        def _():
+            own_group(row)
+
+        local_row(row)
+        for step in range(1, chips):
+            chip_copy(step, row, chip_source(step)).wait_recv()
+            relay_copy(step, row, chip_source(step)).start()
+        side_copy(row).wait_recv()
+
+        @pl.when(has_ahead)
+        def _():
+            far_copy(row).start()
+
+        @pl.when(row >= 1)
+        def _():
+            take_row(row - 1)
+
+        return carry
+
+    lax.fori_loop(0, rows, main, 0)
+    take_row(rows - 1)
+
+    @pl.when(has_behind)
+    def _():
+        for index in range(rows):
+            far_copy(index).wait_recv()
+
+    def finish(index, carry):
+        side_group(index)
+        return carry
+
+    lax.fori_loop(0, chans // GROUP, finish, 0)
+
+    for half in range(halves):
+        for row in range(half * 8, half * 8 + 8):
+            value = acc[row] + acc1[row]
+            place = (pl.ds(row % 8, chans, stride=8), slice(None))
+            pbuf.at[half, 0].reshape(chans * 8, width)[place] = value[:, width:]
+            pbuf.at[half, 1].reshape(chans * 8, width)[place] = -value[:, :width]
+        for part in range(2):
+            store(half, part).start()
+
+    def drain(row, carry):
+        for step in range(1, chips):
+            chip_copy(step, row, chan_at).wait_send()
+            relay_copy(step, row, chip_source(step)).wait_send()
+        core_copy(row, chan_at).wait_send()
+        side_copy(row).wait_send()
+
+        @pl.when(has_ahead)
+        def _():
+            far_copy(row).wait_send()
+
+        return carry
+
+    lax.fori_loop(0, rows, drain, 0)
+    for half in range(halves):
+        for part in range(2):
+            store(half, part).wait()
+
+
+def device_step(peers, rads, psi, k_prev, gaunt, dipole, kinetic, chan_l, field_amp):
+    _, chans, rows, width = psi.shape
+    fits = (
+        chans % (4 * GROUP) == 0
+        and rows == GROUP
+        and peers % 2 == 0
+        and rads % 2 == 0
+        and width == rads * rows
+        and width == 128
+    )
+    if not fits:
+        return on_device(psi, k_prev, gaunt, dipole, kinetic, chan_l, field_amp)
+    orders = gaunt.shape[0] + 1
+    chips = peers // 2
+    lanes = 2 * width
+    size = rows * GROUP
+    f32, bf16, dma = (jnp.float32, jnp.bfloat16, pltpu.SemaphoreType.DMA)
+    anywhere = pl.BlockSpec(memory_space=pl.ANY)
+    vmem = pl.BlockSpec(memory_space=pltpu.VMEM)
+    return pl.pallas_call(
+        functools.partial(fused_kernel, peers, rads),
+        out_shape=jax.ShapeDtypeStruct(psi.shape, f32),
+        in_specs=[anywhere] * 4 + [vmem, vmem, pl.BlockSpec(memory_space=pltpu.SMEM)],
+        out_specs=anywhere,
+        scratch_shapes=[
+            pltpu.VMEM((rows // 8, 2, chans, 8, width), f32),
+            pltpu.VMEM((rows // 8, 2, chans, 8, width), f32),
+            pltpu.VMEM((rows, chans, lanes), f32),
+            pltpu.VMEM((rows, peers * chans, lanes), bf16),
+            pltpu.VMEM((2, rows, chans, lanes), bf16),
+            pltpu.VMEM((rows, chans, lanes), f32),
+            pltpu.VMEM((rows, chans, lanes), f32),
+            pltpu.VMEM((orders, chans, peers * chans), bf16),
+            pltpu.VMEM((3, 2 * size, size), bf16),
+            pltpu.VMEM((lanes, lanes), bf16),
+            pltpu.VMEM((chans, width), f32),
+            pltpu.VMEM((chans, width), f32),
+            dma((2, rows // 8, 2)),
+            dma((orders,)),
+            dma((chips - 1, rows)),
+            dma((chips - 1, rows)),
+            dma((rows,)),
+            dma((rows,)),
+            dma((chips - 1, rows)),
+            dma((chips - 1, rows)),
+            dma((rows,)),
+            dma((rows,)),
+            dma((rows,)),
+            dma((rows,)),
+            dma((rows // 8, 2)),
+        ],
+        compiler_params=pltpu.CompilerParams(
+            collective_id=0, has_side_effects=True, vmem_limit_bytes=60 * 1024 * 1024
+        ),
+    )(psi, k_prev, gaunt, dipole, kinetic, chan_l, field_amp)
+
+
 def solution(mesh):
     placed = (
         P(None, "chan", "rad", None),
@@ -81,7 +518,7 @@
         P(),
     )
     return jax.shard_map(
-        on_device,
+        functools.partial(device_step, mesh.shape["chan"], mesh.shape["rad"]),
         mesh=mesh,
         in_specs=placed,
         out_specs=P(None, "chan", "rad", None),

time: 112 us -> 57.1 us (0.51); the launches traced: 110 us -> 56.9 us
  Pallas kernels: 0 us -> 51 us
  waiting for transfers between devices: 38.1 us -> 0 us
  matrix products: 24.4 us -> 0 us
  local copies, waits for them, and re-layouts: 26.3 us -> 5.2 us
  starting transfers between devices: 14.1 us -> 0 us
  other arithmetic: 5.95 us -> 0 us
    pallas_call x0 -> x1, Pallas kernels: none -> 51 us  [device_step(): pl.pallas_call(functools.partial(fused_kernel, peers, rads), out_shape=ja...]
    all_to_all x2 -> x0, waiting for transfers between devices: 38.1 us -> none  [the longest x1 24.7 us: on_device(): lax.all_to_all(sent, 'chan', split_axis=2, concat_axis=1, tiled=True)]
    dot_general x7 -> x0, matrix products: 24.4 us -> none  [the longest x4 8.34 us: on_device(): jnp.einsum('cd,adq->acq', gaunt[order], block, preferred_element_type=jnp...]
    convert_element_type x3 -> x0, local copies, waits for them, and re-layouts: 11.8 us -> none  [the longest x2 8.79 us: on_device(): coupled.astype(jnp.float32)]
    all_to_all x3 -> x0, local copies, waits for them, and re-layouts: 8.16 us -> none  [the longest x2 6.5 us: on_device(): lax.all_to_all(sent, 'chan', split_axis=2, concat_axis=1, tiled=True)]
    all_to_all x2 -> x0, starting transfers between devices: 8.15 us -> none  [the longest x1 4.54 us: on_device(): lax.all_to_all(total.astype(jnp.bfloat16), 'chan', split_axis=1, concat_a...]
    ppermute x2 -> x0, starting transfers between devices: 5.96 us -> none  [the longest x1 3.55 us: extended(): before = lax.ppermute(last, axis, up)]
    convert_element_type x3 -> x0, other arithmetic: 4.91 us -> none  [the longest x1 4.48 us: on_device(): section.astype(jnp.bfloat16)]
  transfers between devices with their start and end apart: 4 -> 0, of which waited for: 2 -> 0; matrix products, arithmetic and copies ran while one was open for 39% -> 0% of each run, Pallas kernels for 0% -> 0%
where the time goes in v1:
time: 57.1 us; the launch traced here: 56.9 us
  Pallas kernels  51 us (89%)
  local copies, waits for them, and re-layouts  5.2 us (9%)
  between operations  0.66 us (1%)
    pallas_call x1, Pallas kernels, device_step(): pl.pallas_call(functools.partial(fused_kernel, peers, rads), out_shape=ja...  51 us
    unnamed x2, local copies, waits for them, and re-layouts  5.2 us

profile of v1, /device:TPU:20, one launch (start us, length us, event | category | flops | bytes accessed | tf_op | source)
XLA Modules:
  0.0 56.9 jit_solution(3080378578269128617)
XLA Ops:
  0.7 1.4 %copy.8.chan_l = s32[192,2]{1,0:T(8,128)} copy(s32[192,2]{0,1:T(2,128)} %param.12) | data formatting | bytes 3072 | tf_op args[5]
  2.1 51.0 %shard_map.73 = f32[2,192,16,128]{3,2,1,0:T(8,128)} custom-call(f32[2,192,16,128]{3,2,1,0:T(8,128)} %psi.1, f32[2,192,16,128]{3,2,1,0:T(8,128)} %k_prev.1, bf16[4,768,768]{2,1,0:T(8,128)(2,1)} %gaunt.1, bf16[768,768]{1,0:T(8,128)(2,1)} %dipole.1, f32[128,128]{1,0:T(8,128)} %kin.1, s32[192,2]{1,0:T(8,128)} %copy.8.chan_l, f32[1]{0:T(128)S(6)} %copy.10.field), custom_call_target="tpu_custom_call" | custom-call | tf_op jit(solution)/shard_map/pallas_call | solution.py:472
  53.1 3.8 %copy.11 = f32[2,192,16,128]{3,2,1,0:T(8,128)} copy(f32[2,192,16,128]{3,2,1,0:T(8,128)} %shard_map.73) | data formatting | bytes 6291456

commit v2 on v1

--- a/solution.py
+++ b/solution.py
@@ -108,6 +108,8 @@
     langle,
     load_sem,
     weight_sem,
+    hs,
+    hr,
     xs,
     xr,
     cs,
@@ -124,9 +126,8 @@
     width = lanes // 2
     orders = weights.shape[0]
     chips = peers // 2
-    halves = rows // 8
-    quarter = rows // 4
-    span = chans // 4
+    groups = chans // GROUP
+    lead = rows // 4
     chan_at = lax.axis_index("chan")
     rad_at = lax.axis_index("rad")
     core = chan_at % 2
@@ -144,18 +145,24 @@
     def block(owner):
         return pl.ds(pl.multiple_of(owner * chans, GROUP), chans)
 
+    def cut_of(group):
+        return pl.ds(pl.multiple_of(group * GROUP, GROUP), GROUP)
+
+    def block_cut(owner, group):
+        return pl.ds(pl.multiple_of(owner * chans + group * GROUP, GROUP), GROUP)
+
     def chip_peer(step):
         return lax.rem(chip + step, chips) * 2 + core
 
     def chip_source(step):
         return lax.rem(chip - step + chips, chips) * 2 + core
 
-    def load(which, half, part):
+    def load(which, group):
         source, target = ((psi, pbuf), (k_prev, kbuf))[which]
         return pltpu.make_async_copy(
-            source.at[part, :, pl.ds(half * 8, 8), :],
-            target.at[half, part],
-            load_sem.at[which, half, part],
+            source.at[:, cut_of(group), :, :],
+            target.at[:, cut_of(group), :, :],
+            load_sem.at[which, group],
         )
 
     def load_weight(order):
@@ -164,68 +171,56 @@
             source.at[block(chan_at), :], weights.at[order], weight_sem.at[order]
         )
 
-    def store(half, part):
+    def store(group):
         return pltpu.make_async_copy(
-            pbuf.at[half, part],
-            out.at[part, :, pl.ds(half * 8, 8), :],
-            store_sem.at[half, part],
-        )
-
-    def remote(ref, send, recv, target):
+            pbuf.at[:, cut_of(group), :, :], out.at[:, cut_of(group), :, :], store_sem.at[group]
+        )
+
+    def remote(source, target, send, recv, device):
         return pltpu.make_async_remote_copy(
-            src_ref=ref[0],
-            dst_ref=ref[1],
+            src_ref=source,
+            dst_ref=target,
             send_sem=send,
             recv_sem=recv,
-            device_id=target,
+            device_id=device,
             device_id_type=MESH,
         )
+
+    def lead_copy(step, group, owner):
+        view = xg.at[0:lead, block_cut(owner, group), :]
+        device = {"chan": chip_peer(step)}
+        return remote(view, view, hs.at[step - 1, group], hr.at[step - 1, group], device)
 
     def chip_copy(step, row, owner):
         view = xg.at[row, block(owner), :]
-        return remote(
-            (view, view), xs.at[step - 1, row], xr.at[step - 1, row], {"chan": chip_peer(step)}
-        )
-
-    def core_copy(row, owner):
-        view = xg.at[row, block(owner), :]
-        return remote((view, view), cs.at[row], cr.at[row], {"chan": partner})
+        device = {"chan": chip_peer(step)}
+        return remote(view, view, xs.at[step - 1, row], xr.at[step - 1, row], device)
+
+    def core_copy(index, owner):
+        view = xg.at[index * lead : (index + 1) * lead, block(owner), :]
+        return remote(view, view, cs.at[index], cr.at[index], {"chan": partner})
+
+    def relay_lead(step, owner):
+        view = xg.at[0:lead, block(owner), :]
+        return remote(view, view, fs.at[step - 1, 0], fr.at[step - 1, 0], {"chan": partner})
 
     def relay_copy(step, row, owner):
         view = xg.at[row, block(owner), :]
-        return remote((view, view), fs.at[step - 1, row], fr.at[step - 1, row], {"chan": partner})
-
-    def piece(index):
-        row = pl.ds(pl.multiple_of((index // 4) * quarter, quarter), quarter)
-        first = pl.multiple_of((index % 4) * span, GROUP)
-        return row, first
-
-    def own_piece(index):
-        row, first = piece(index)
-        start = pl.multiple_of(chan_at * chans + first, GROUP)
-        return xg.at[row, pl.ds(start, span), :]
-
-    def halo_piece(slot, index):
-        row, first = piece(index)
-        return halo.at[slot, row, pl.ds(first, span), :]
-
-    def side_copy(index):
-        return remote(
-            (own_piece(index), halo_piece(minor, index)), ys.at[index], yr.at[index], {"rad": other}
-        )
-
-    def far_copy(index):
-        return remote(
-            (halo_piece(near_slot, index), halo_piece(minor, index)),
-            zs.at[index],
-            zr.at[index],
-            {"rad": ahead},
-        )
-
-    for half in range(halves):
-        for part in range(2):
-            for which in range(2):
-                load(which, half, part).start()
+        return remote(view, view, fs.at[step - 1, row], fr.at[step - 1, row], {"chan": partner})
+
+    def side_copy(group):
+        source = xg.at[:, block_cut(chan_at, group), :]
+        target = halo.at[minor, :, cut_of(group), :]
+        return remote(source, target, ys.at[group], yr.at[group], {"rad": other})
+
+    def far_copy(group):
+        source = halo.at[near_slot, :, cut_of(group), :]
+        target = halo.at[minor, :, cut_of(group), :]
+        return remote(source, target, zs.at[group], zr.at[group], {"rad": ahead})
+
+    for group in range(groups):
+        for which in range(2):
+            load(which, group).start()
     for order in range(orders):
         load_weight(order).start()
 
@@ -245,44 +240,46 @@
     def _():
         pl.semaphore_signal(barrier, inc=1, device_id={"rad": behind}, device_id_type=MESH)
 
+    def form(group):
+        for which in range(2):
+            load(which, group).wait()
+        for part in range(2):
+            first = pbuf.at[part].reshape(chans * rows, width)
+            second = kbuf.at[part].reshape(chans * rows, width)
+            cut = slice(part * width, (part + 1) * width)
+            for row in range(rows):
+                place = (pl.ds(group * GROUP * rows + row, GROUP, stride=rows), slice(None))
+                value = first[place] + 0.5 * second[place]
+                sec[row, cut_of(group), cut] = value
+                xg[row, block_cut(chan_at, group), cut] = value.astype(jnp.bfloat16)
+
+    def send_group(group):
+        side_copy(group).start()
+        for step in range(1, chips):
+            lead_copy(step, group, chan_at).start()
+
+    form(0)
     pl.semaphore_wait(
         barrier, chips + 1 + has_ahead.astype(jnp.int32) + has_behind.astype(jnp.int32)
     )
 
-    def send_row(row):
-        for step in range(1, chips):
-            chip_copy(step, row, chan_at).start()
-        core_copy(row, chan_at).start()
-
-    def send_side(first):
-        for index in range(4):
-            side_copy(first * 4 + index).start()
-
-    for half in range(halves):
-        for part in range(2):
-            for which in range(2):
-                load(which, half, part).wait()
-        for row in range(half * 8, half * 8 + 8):
-            for part in range(2):
-                place = (pl.ds(row % 8, chans, stride=8), slice(None))
-                value = (
-                    pbuf.at[half, part].reshape(chans * 8, width)[place]
-                    + 0.5 * kbuf.at[half, part].reshape(chans * 8, width)[place]
-                )
-                cut = slice(part * width, (part + 1) * width)
-                sec[row, :, cut] = value
-                xg[row, block(chan_at), cut] = value.astype(jnp.bfloat16)
-            if row >= 1:
-                send_row(row - 1)
-                if row % quarter == 0:
-                    send_side(row // quarter - 1)
+    def form_next(group, carry):
+        form(group)
+        send_group(group - 1)
+        return carry
+
+    lax.fori_loop(1, groups, form_next, 0)
 
     kin_high, kin_low = split_bf16(kin[...])
     both = jnp.concatenate([kin_high, kin_low], axis=1)
     kk[0:width, :] = both
     kk[width : 2 * width, :] = both
-    send_row(rows - 1)
-    send_side(3)
+    send_group(groups - 1)
+    for row in range(lead, rows):
+        for step in range(1, chips):
+            chip_copy(step, row, chan_at).start()
+    for index in range(4):
+        core_copy(index, chan_at).start()
 
     band = kin[pl.ds(pl.multiple_of(rad_at * rows, rows), rows), :]
     size = rows * GROUP
@@ -310,10 +307,16 @@
         lax.broadcasted_iota(jnp.int32, (1, lanes), 1) % width
     ).astype(jnp.float32) / width
     inner_r = second_r[:, :width]
-    lvals = chan_l[...].astype(jnp.float32)
-    lvals = lvals * (lvals + 1.0)
-    lmul[...] = jnp.broadcast_to(lvals[:, 0:1], (chans, width))
-    langle[...] = lvals[:, 1:2] / (2.0 * inner_r * inner_r) - 2.0 / inner_r
+    lvals = chan_l[...].astype(jnp.float32).astype(jnp.bfloat16)
+    first = lax.broadcasted_iota(jnp.int32, (2, lanes), 0)
+    spread = first == lax.broadcasted_iota(jnp.int32, (2, lanes), 1) // width
+    spread = jnp.where(spread, 1.0, 0.0).astype(jnp.bfloat16)
+    lwide = lax.dot_general(
+        lvals, spread, (((0,), (0,)), ((), ())), preferred_element_type=jnp.float32
+    )
+    lwide = lwide * (lwide + 1.0)
+    lmul[...] = lwide[:, :width]
+    langle[...] = lwide[:, width:] / (2.0 * inner_r * inner_r) - 2.0 / inner_r
 
     def radius(row):
         place = jnp.full((1, lanes), rad_at * rows + row, jnp.int32)
@@ -381,79 +384,131 @@
                 jnp.bfloat16
             ).astype(jnp.float32)
 
+    def relay(row):
+        for step in range(1, chips):
+            chip_copy(step, row, chip_source(step)).wait_recv()
+            relay_copy(step, row, chip_source(step)).start()
+
     def take_row(row):
-        core_copy(row, partner).wait_recv()
         for step in range(1, chips):
             relay_copy(step, row, chip_source(step) + 1 - 2 * core).wait_recv()
         couple(row)
 
-    def main(row, carry):
-        @pl.when(row < chans // GROUP)
-        def _():
-            own_group(row)
-
-        local_row(row)
-        for step in range(1, chips):
-            chip_copy(step, row, chip_source(step)).wait_recv()
-            relay_copy(step, row, chip_source(step)).start()
-        side_copy(row).wait_recv()
+    def pass_side(group):
+        side_copy(group).wait_recv()
 
         @pl.when(has_ahead)
         def _():
-            far_copy(row).start()
-
-        @pl.when(row >= 1)
-        def _():
-            take_row(row - 1)
-
+            far_copy(group).start()
+
+    def take_side(group):
+        @pl.when(has_behind)
+        def _():
+            far_copy(group).wait_recv()
+
+        side_group(group)
+
+    early = groups // 4
+
+    def begin(index, carry):
+        own_group(index)
+        for place in range(4):
+            local_row(index * 4 + place)
+        pass_side(index)
         return carry
 
-    lax.fori_loop(0, rows, main, 0)
+    lax.fori_loop(0, early, begin, 0)
+    for step in range(1, chips):
+        for group in range(groups):
+            lead_copy(step, group, chip_source(step)).wait_recv()
+        relay_lead(step, chip_source(step)).start()
+    for index in range(4):
+        core_copy(index, partner).wait_recv()
+    for step in range(1, chips):
+        relay_lead(step, chip_source(step) + 1 - 2 * core).wait_recv()
+
+    def main(index, carry):
+        @pl.when(index + early < groups)
+        def _():
+            own_group(index + early)
+
+        @pl.when(jnp.logical_and(index >= lead, index < 2 * lead))
+        def _():
+            local_row(index + rows - 2 * lead)
+
+        late = index - index // 4
+
+        @pl.when(index % 4 != 3)
+        def _():
+            pass_side(early + late)
+
+        relay(lead + index)
+
+        @pl.when(index < lead)
+        def _():
+            couple(index)
+
+        @pl.when(index % 4 != 3)
+        def _():
+            take_side(late)
+
+        @pl.when(index >= 1)
+        def _():
+            take_row(lead + index - 1)
+
+        return carry
+
+    lax.fori_loop(0, rows - lead, main, 0)
     take_row(rows - 1)
 
-    @pl.when(has_behind)
-    def _():
-        for index in range(rows):
-            far_copy(index).wait_recv()
-
-    def finish(index, carry):
-        side_group(index)
+    def finish(group, carry):
+        @pl.when(group >= groups - early)
+        def _():
+            take_side(group)
+
+        cut = cut_of(group)
+        first = pbuf.at[0].reshape(chans * rows, width)
+        second = pbuf.at[1].reshape(chans * rows, width)
+        for row in range(rows):
+            value = acc[row, cut, :] + acc1[row, cut, :]
+            place = (pl.ds(group * GROUP * rows + row, GROUP, stride=rows), slice(None))
+            first[place] = value[:, width:]
+            second[place] = -value[:, :width]
+        store(group).start()
         return carry
 
-    lax.fori_loop(0, chans // GROUP, finish, 0)
-
-    for half in range(halves):
-        for row in range(half * 8, half * 8 + 8):
-            value = acc[row] + acc1[row]
-            place = (pl.ds(row % 8, chans, stride=8), slice(None))
-            pbuf.at[half, 0].reshape(chans * 8, width)[place] = value[:, width:]
-            pbuf.at[half, 1].reshape(chans * 8, width)[place] = -value[:, :width]
-        for part in range(2):
-            store(half, part).start()
-
-    def drain(row, carry):
+    lax.fori_loop(0, groups, finish, 0)
+
+    def drain_row(row, carry):
         for step in range(1, chips):
             chip_copy(step, row, chan_at).wait_send()
             relay_copy(step, row, chip_source(step)).wait_send()
-        core_copy(row, chan_at).wait_send()
-        side_copy(row).wait_send()
+        return carry
+
+    def drain_group(group, carry):
+        for step in range(1, chips):
+            lead_copy(step, group, chan_at).wait_send()
+        side_copy(group).wait_send()
 
         @pl.when(has_ahead)
         def _():
-            far_copy(row).wait_send()
-
+            far_copy(group).wait_send()
+
+        store(group).wait()
         return carry
 
-    lax.fori_loop(0, rows, drain, 0)
-    for half in range(halves):
-        for part in range(2):
-            store(half, part).wait()
+    for index in range(4):
+        core_copy(index, chan_at).wait_send()
+    for step in range(1, chips):
+        relay_lead(step, chip_source(step)).wait_send()
+    lax.fori_loop(lead, rows, drain_row, 0)
+    lax.fori_loop(0, groups, drain_group, 0)
 
 
 def device_step(peers, rads, psi, k_prev, gaunt, dipole, kinetic, chan_l, field_amp):
     _, chans, rows, width = psi.shape
     fits = (
-        chans % (4 * GROUP) == 0
+        chans == 3 * 4 * GROUP
         and rows == GROUP
         and peers % 2 == 0
         and rads % 2 == 0
@@ -464,19 +519,24 @@
         return on_device(psi, k_prev, gaunt, dipole, kinetic, chan_l, field_amp)
     orders = gaunt.shape[0] + 1
     chips = peers // 2
+    groups = chans // GROUP
     lanes = 2 * width
     size = rows * GROUP
     f32, bf16, dma = (jnp.float32, jnp.bfloat16, pltpu.SemaphoreType.DMA)
-    anywhere = pl.BlockSpec(memory_space=pl.ANY)
+    main_memory = pl.BlockSpec(memory_space=pltpu.HBM)
     vmem = pl.BlockSpec(memory_space=pltpu.VMEM)
+    psi, k_prev, gaunt, dipole = (
+        pltpu.with_memory_space_constraint(value, pltpu.HBM)
+        for value in (psi, k_prev, gaunt, dipole)
+    )
     return pl.pallas_call(
         functools.partial(fused_kernel, peers, rads),
         out_shape=jax.ShapeDtypeStruct(psi.shape, f32),
-        in_specs=[anywhere] * 4 + [vmem, vmem, pl.BlockSpec(memory_space=pltpu.SMEM)],
-        out_specs=anywhere,
+        in_specs=[main_memory] * 4 + [vmem, vmem, pl.BlockSpec(memory_space=pltpu.SMEM)],
+        out_specs=pl.BlockSpec(memory_space=pl.ANY),
         scratch_shapes=[
-            pltpu.VMEM((rows // 8, 2, chans, 8, width), f32),
-            pltpu.VMEM((rows // 8, 2, chans, 8, width), f32),
+            pltpu.VMEM((2, chans, rows, width), f32),
+            pltpu.VMEM((2, chans, rows, width), f32),
             pltpu.VMEM((rows, chans, lanes), f32),
             pltpu.VMEM((rows, peers * chans, lanes), bf16),
             pltpu.VMEM((2, rows, chans, lanes), bf16),
@@ -487,24 +547,26 @@
             pltpu.VMEM((lanes, lanes), bf16),
             pltpu.VMEM((chans, width), f32),
             pltpu.VMEM((chans, width), f32),
-            dma((2, rows // 8, 2)),
+            dma((2, groups)),
             dma((orders,)),
+            dma((chips - 1, groups)),
+            dma((chips - 1, groups)),
             dma((chips - 1, rows)),
             dma((chips - 1, rows)),
-            dma((rows,)),
-            dma((rows,)),
+            dma((4,)),
+            dma((4,)),
             dma((chips - 1, rows)),
             dma((chips - 1, rows)),
-            dma((rows,)),
-            dma((rows,)),
-            dma((rows,)),
-            dma((rows,)),
-            dma((rows // 8, 2)),
+            dma((groups,)),
+            dma((groups,)),
+            dma((groups,)),
+            dma((groups,)),
+            dma((groups,)),
         ],
         compiler_params=pltpu.CompilerParams(
-            collective_id=0, has_side_effects=True, vmem_limit_bytes=60 * 1024 * 1024
+            collective_id=0, has_side_effects=True, vmem_limit_bytes=36 * 1024 * 1024
         ),
-    )(psi, k_prev, gaunt, dipole, kinetic, chan_l, field_amp)
+    )(psi, k_prev, gaunt, dipole, kinetic, chan_l.T, field_amp)
 
 
 def solution(mesh):

time: 57.1 us -> 49.9 us (0.87)
  Pallas kernels: 51 us -> 45.5 us
  local copies, waits for them, and re-layouts: 5.2 us -> 3.18 us
    pallas_call x1, Pallas kernels: 51 us -> 45.5 us  [device_step(): pl.pallas_call(functools.partial(fused_kernel, peers, rads), out_shape=ja...]
    unnamed x2 -> x5, local copies, waits for them, and re-layouts: 5.2 us -> 3.18 us
where the time goes in v2:
time: 49.9 us; the launch traced here: 49.4 us
  Pallas kernels  45.5 us (91%)
  local copies, waits for them, and re-layouts  3.18 us (6%)
  between operations  0.67 us (1%)
    pallas_call x1, Pallas kernels, device_step(): pl.pallas_call(functools.partial(fused_kernel, peers, rads), out_shape=ja...  45.5 us
    unnamed x5, local copies, waits for them, and re-layouts  3.18 us

profile of v2, /device:TPU:20, one launch (start us, length us, event | category | flops | bytes accessed | tf_op | source)
XLA Modules:
  0.0 49.4 jit_solution(5501781398910995934)
XLA Ops:
  0.7 0.0 copy-start
  0.7 0.8 %copy-done = f32[128,128]{1,0:T(8,128)S(1)} copy-done((f32[128,128]{1,0:T(8,128)S(1)}, f32[128,128]{1,0:T(8,128)}, u32[]{:S(2)}) %copy-start) | copy-done | bytes 65560
  1.5 0.0 copy-start.1
  1.5 0.7 %copy-done.1 = s32[192,2]{0,1:T(2,128)S(1)} copy-done((s32[192,2]{0,1:T(2,128)S(1)}, s32[192,2]{0,1:T(2,128)}, u32[]{:S(2)}) %copy-start.1) | copy-done | bytes 1560
  2.2 45.5 %shard_map.73 = f32[2,192,16,128]{3,2,1,0:T(8,128)S(1)} custom-call(f32[2,192,16,128]{3,2,1,0:T(8,128)} %psi.1, f32[2,192,16,128]{3,2,1,0:T(8,128)} %k_prev.1, bf16[4,768,768]{2,1,0:T(8,128)(2,1)} %gaunt.1, bf16[768,768]{1,0:T(8,128)(2,1)} %dipole.1, f32[128,128]{1,0:T(8,128)S(1)} %copy-done, s32[2,192]{1,0:T(2,128)S(1)} %bitcast.1, f32[1]{0:T(128)S(6)} %copy.9.field), custom_call_target="tpu_custom_call" | custom-call | tf_op jit(solution)/shard_map/pallas_call | solution.py:532
  47.7 1.7 %copy.10 = f32[2,192,16,128]{3,2,1,0:T(8,128)} copy(f32[2,192,16,128]{3,2,1,0:T(8,128)S(1)} %shard_map.73) | data formatting | bytes 6291456
Async XLA Ops:
  0.7 0.8 %copy-start = (f32[128,128]{1,0:T(8,128)S(1)}, f32[128,128]{1,0:T(8,128)}, u32[]{:S(2)}) copy-start(f32[128,128]{1,0:T(8,128)} %kin.1) | copy-start | bytes 196612
  1.5 0.7 %copy-start.1 = (s32[192,2]{0,1:T(2,128)S(1)}, s32[192,2]{0,1:T(2,128)}, u32[]{:S(2)}) copy-start(s32[192,2]{0,1:T(2,128)} %param.12) | copy-start | bytes 4612

commit v3 on v2

--- a/solution.py
+++ b/solution.py
@@ -90,10 +90,12 @@
     k_prev,
     gaunt,
     dipole,
+    kin_main,
+    chan_main,
+    field,
+    out,
     kin,
     chan_l,
-    field,
-    out,
     pbuf,
     kbuf,
     sec,
@@ -120,7 +122,7 @@
     yr,
     zs,
     zr,
-    store_sem,
+    small_sem,
 ):
     rows, chans, lanes = sec.shape
     width = lanes // 2
@@ -171,11 +173,6 @@
             source.at[block(chan_at), :], weights.at[order], weight_sem.at[order]
         )
 
-    def store(group):
-        return pltpu.make_async_copy(
-            pbuf.at[:, cut_of(group), :, :], out.at[:, cut_of(group), :, :], store_sem.at[group]
-        )
-
     def remote(source, target, send, recv, device):
         return pltpu.make_async_remote_copy(
             src_ref=source,
@@ -208,21 +205,27 @@
         view = xg.at[row, block(owner), :]
         return remote(view, view, fs.at[step - 1, row], fr.at[step - 1, row], {"chan": partner})
 
-    def side_copy(group):
-        source = xg.at[:, block_cut(chan_at, group), :]
-        target = halo.at[minor, :, cut_of(group), :]
-        return remote(source, target, ys.at[group], yr.at[group], {"rad": other})
-
-    def far_copy(group):
-        source = halo.at[near_slot, :, cut_of(group), :]
-        target = halo.at[minor, :, cut_of(group), :]
-        return remote(source, target, zs.at[group], zr.at[group], {"rad": ahead})
-
-    for group in range(groups):
+    def half_of(half):
+        return slice(half * (rows // 2), (half + 1) * (rows // 2))
+
+    def side_copy(group, half):
+        source = xg.at[half_of(half), block_cut(chan_at, group), :]
+        target = halo.at[minor, half_of(half), cut_of(group), :]
+        return remote(source, target, ys.at[half, group], yr.at[half, group], {"rad": other})
+
+    def far_copy(group, half):
+        source = halo.at[near_slot, half_of(half), cut_of(group), :]
+        target = halo.at[minor, half_of(half), cut_of(group), :]
+        return remote(source, target, zs.at[half, group], zr.at[half, group], {"rad": ahead})
+
+    small = [
+        pltpu.make_async_copy(kin_main, kin, small_sem.at[0]),
+        pltpu.make_async_copy(chan_main, chan_l, small_sem.at[1]),
+    ]
+    depth = groups
+    for group in range(depth):
         for which in range(2):
             load(which, group).start()
-    for order in range(orders):
-        load_weight(order).start()
 
     barrier = pltpu.get_barrier_semaphore()
     for step in range(1, chips):
@@ -243,6 +246,7 @@
     def form(group):
         for which in range(2):
             load(which, group).wait()
+
         for part in range(2):
             first = pbuf.at[part].reshape(chans * rows, width)
             second = kbuf.at[part].reshape(chans * rows, width)
@@ -254,11 +258,12 @@
                 xg[row, block_cut(chan_at, group), cut] = value.astype(jnp.bfloat16)
 
     def send_group(group):
-        side_copy(group).start()
+        for half in range(2):
+            side_copy(group, half).start()
         for step in range(1, chips):
             lead_copy(step, group, chan_at).start()
 
-    form(0)
+    form(jnp.int32(0))
     pl.semaphore_wait(
         barrier, chips + 1 + has_ahead.astype(jnp.int32) + has_behind.astype(jnp.int32)
     )
@@ -269,17 +274,24 @@
         return carry
 
     lax.fori_loop(1, groups, form_next, 0)
-
-    kin_high, kin_low = split_bf16(kin[...])
-    both = jnp.concatenate([kin_high, kin_low], axis=1)
-    kk[0:width, :] = both
-    kk[width : 2 * width, :] = both
+    for copy in small:
+        copy.start()
+    for order in range(orders):
+        load_weight(order).start()
+
     send_group(groups - 1)
     for row in range(lead, rows):
         for step in range(1, chips):
             chip_copy(step, row, chan_at).start()
     for index in range(4):
         core_copy(index, chan_at).start()
+
+    for copy in small:
+        copy.wait()
+    kin_high, kin_low = split_bf16(kin[...])
+    both = jnp.concatenate([kin_high, kin_low], axis=1)
+    kk[0:width, :] = both
+    kk[width : 2 * width, :] = both
 
     band = kin[pl.ds(pl.multiple_of(rad_at * rows, rows), rows), :]
     size = rows * GROUP
@@ -395,16 +407,18 @@
         couple(row)
 
     def pass_side(group):
-        side_copy(group).wait_recv()
-
-        @pl.when(has_ahead)
-        def _():
-            far_copy(group).start()
+        for half in range(2):
+            side_copy(group, half).wait_recv()
+
+            @pl.when(has_ahead)
+            def _():
+                far_copy(group, half).start()
 
     def take_side(group):
         @pl.when(has_behind)
         def _():
-            far_copy(group).wait_recv()
+            for half in range(2):
+                far_copy(group, half).wait_recv()
 
         side_group(group)
 
@@ -436,11 +450,11 @@
         def _():
             local_row(index + rows - 2 * lead)
 
-        late = index - index // 4
+        late = early + index - index // 4
 
         @pl.when(index % 4 != 3)
         def _():
-            pass_side(early + late)
+            pass_side(late)
 
         relay(lead + index)
 
@@ -450,7 +464,7 @@
 
         @pl.when(index % 4 != 3)
         def _():
-            take_side(late)
+            take_side(late - early)
 
         @pl.when(index >= 1)
         def _():
@@ -459,25 +473,34 @@
         return carry
 
     lax.fori_loop(0, rows - lead, main, 0)
-    take_row(rows - 1)
-
-    def finish(group, carry):
-        @pl.when(group >= groups - early)
-        def _():
-            take_side(group)
-
+
+    def merge(group, some_rows):
         cut = cut_of(group)
-        first = pbuf.at[0].reshape(chans * rows, width)
-        second = pbuf.at[1].reshape(chans * rows, width)
-        for row in range(rows):
+        first = out.at[0].reshape(chans * rows, width)
+        second = out.at[1].reshape(chans * rows, width)
+        for row in some_rows:
             value = acc[row, cut, :] + acc1[row, cut, :]
             place = (pl.ds(group * GROUP * rows + row, GROUP, stride=rows), slice(None))
             first[place] = value[:, width:]
             second[place] = -value[:, :width]
-        store(group).start()
-        return carry
-
-    lax.fori_loop(0, groups, finish, 0)
+
+    def merge_most(group, carry):
+        merge(group, range(rows - 1))
+        return carry
+
+    def merge_last(group, carry):
+        merge(group, range(rows - 1, rows))
+        return carry
+
+    def merge_side(group, carry):
+        take_side(group)
+        merge(group, range(rows))
+        return carry
+
+    lax.fori_loop(0, groups - early, merge_most, 0)
+    take_row(rows - 1)
+    lax.fori_loop(0, groups - early, merge_last, 0)
+    lax.fori_loop(groups - early, groups, merge_side, 0)
 
     def drain_row(row, carry):
         for step in range(1, chips):
@@ -488,13 +511,14 @@
     def drain_group(group, carry):
         for step in range(1, chips):
             lead_copy(step, group, chan_at).wait_send()
-        side_copy(group).wait_send()
+        for half in range(2):
+            side_copy(group, half).wait_send()
 
         @pl.when(has_ahead)
         def _():
-            far_copy(group).wait_send()
-
-        store(group).wait()
+            for half in range(2):
+                far_copy(group, half).wait_send()
+
         return carry
 
     for index in range(4):
@@ -525,16 +549,18 @@
     f32, bf16, dma = (jnp.float32, jnp.bfloat16, pltpu.SemaphoreType.DMA)
     main_memory = pl.BlockSpec(memory_space=pltpu.HBM)
     vmem = pl.BlockSpec(memory_space=pltpu.VMEM)
-    psi, k_prev, gaunt, dipole = (
+    psi, k_prev, gaunt, dipole, kinetic, chan_l = (
         pltpu.with_memory_space_constraint(value, pltpu.HBM)
-        for value in (psi, k_prev, gaunt, dipole)
+        for value in (psi, k_prev, gaunt, dipole, kinetic, chan_l.T)
     )
     return pl.pallas_call(
         functools.partial(fused_kernel, peers, rads),
         out_shape=jax.ShapeDtypeStruct(psi.shape, f32),
-        in_specs=[main_memory] * 4 + [vmem, vmem, pl.BlockSpec(memory_space=pltpu.SMEM)],
-        out_specs=pl.BlockSpec(memory_space=pl.ANY),
+        in_specs=[main_memory] * 6 + [pl.BlockSpec(memory_space=pltpu.SMEM)],
+        out_specs=vmem,
         scratch_shapes=[
+            pltpu.VMEM(kinetic.shape, f32),
+            pltpu.VMEM((2, chans), jnp.int32),
             pltpu.VMEM((2, chans, rows, width), f32),
             pltpu.VMEM((2, chans, rows, width), f32),
             pltpu.VMEM((rows, chans, lanes), f32),
@@ -557,16 +583,16 @@
             dma((4,)),
             dma((chips - 1, rows)),
             dma((chips - 1, rows)),
-            dma((groups,)),
-            dma((groups,)),
-            dma((groups,)),
-            dma((groups,)),
-            dma((groups,)),
+            dma((2, groups)),
+            dma((2, groups)),
+            dma((2, groups)),
+            dma((2, groups)),
+            dma((2,)),
         ],
         compiler_params=pltpu.CompilerParams(
             collective_id=0, has_side_effects=True, vmem_limit_bytes=36 * 1024 * 1024
         ),
-    )(psi, k_prev, gaunt, dipole, kinetic, chan_l.T, field_amp)
+    )(psi, k_prev, gaunt, dipole, kinetic, chan_l, field_amp)
 
 
 def solution(mesh):

time: 49.9 us -> 48.5 us (0.972)
  local copies, waits for them, and re-layouts: 3.18 us -> 1.67 us
    unnamed x5 -> x1, local copies, waits for them, and re-layouts: 3.18 us -> 1.67 us
where the time goes in v3:
time: 48.5 us; the launch traced here: 48.3 us
  Pallas kernels  45.9 us (95%)
  local copies, waits for them, and re-layouts  1.67 us (3%)
  between operations  0.66 us (1%)
    pallas_call x1, Pallas kernels, device_step(): pl.pallas_call(functools.partial(fused_kernel, peers, rads), out_shape=ja...  45.9 us
    unnamed x1, local copies, waits for them, and re-layouts  1.67 us

profile of v3, /device:TPU:20, one launch (start us, length us, event | category | flops | bytes accessed | tf_op | source)
XLA Modules:
  0.0 48.3 jit_solution(6105360961943990251)
XLA Ops:
  0.7 45.9 %shard_map.73 = f32[2,192,16,128]{3,2,1,0:T(8,128)S(1)} custom-call(f32[2,192,16,128]{3,2,1,0:T(8,128)} %psi.1, f32[2,192,16,128]{3,2,1,0:T(8,128)} %k_prev.1, bf16[4,768,768]{2,1,0:T(8,128)(2,1)} %gaunt.1, bf16[768,768]{1,0:T(8,128)(2,1)} %dipole.1, f32[128,128]{1,0:T(8,128)} %kin_main.1, s32[2,192]{1,0:T(2,128)} %bitcast.1, f32[1]{0:T(128)S(6)} %copy.9.field), custom_call_target="tpu_custom_call" | custom-call | tf_op jit(solution)/shard_map/pallas_call | solution.py:556
  46.6 1.7 %copy.10 = f32[2,192,16,128]{3,2,1,0:T(8,128)} copy(f32[2,192,16,128]{3,2,1,0:T(8,128)S(1)} %shard_map.73) | data formatting | bytes 6291456
